TPU v7x, 32 devices: a whole 2x2x4 slice. The times are simulated.
32 devices in a mesh: dp: 8 (over y, x, core), expert: 4 (over z).
Axes of the slice: x: 2, y: 2, z: 4, core: 2. Of those that a mesh axis runs over, the one named last changes fastest.
Arguments:
- tokens: bfloat16 [4096, 2048], P(('dp', 'expert')), may hold values from -6 to 6
- w_qkv: bfloat16 [3, 2048, 2048], P(None, 'dp', 'expert'), may hold values from -0.125 to 0.125
- w_out: bfloat16 [2048, 2048], P('expert', 'dp'), may hold values from -0.5 to 0.5
- attention_norm_gain: bfloat16 [2048], P('dp'), may hold values from 0.5 to 1.5
- gain_ffn: bfloat16 [2048], P('dp'), may hold values from 0.5 to 1.5
- w_router: bfloat16 [2048, 4], P('dp'), may hold values from -0.09375 to 0.09375
- w_gate_up: bfloat16 [4, 2048, 11264], P('expert', 'dp'), may hold values from -0.125 to 0.125
- w_down: bfloat16 [4, 5632, 2048], P('expert', 'dp'), may hold values from -0.15625 to 0.15625
- lengths: int32 [8], P('dp'), may hold values from 128 to 512, as said below
- routes: int32 [4096, 2], P(('dp', 'expert')), may hold values from 0 to 3, all different within a row
- order: int32 [4096], P(('dp', 'expert')), may hold values from 0 to 127, as said below
- cotangent: bfloat16 [4096, 2048], P(('dp', 'expert')), may hold values from -6 to 6
Outputs:
- output: bfloat16 [4096, 2048], P(('dp', 'expert'))
- grad_tokens: bfloat16 [4096, 2048], P(('dp', 'expert'))
- grad_qkv: float32 [3, 2048, 2048], P(None, 'dp', 'expert')
- grad_out: float32 [2048, 2048], P('expert', 'dp')
- grad_gain_attn: float32 [2048], P('dp')
- grad_gain_ffn: float32 [2048], P('dp')
- grad_router: float32 [2048, 4], P('dp')
- grad_gate_up: float32 [4, 2048, 11264], P('expert', 'dp')
- grad_down: float32 [4, 5632, 2048], P('expert', 'dp')
Inputs may be any that keep to these rules, and one draw needn't show every extreme that they name: `lengths`: one sequence of every draw has exactly 512 live tokens. `routes`: each token slot names 2 different experts, and every expert is named somewhere. `order`: each aligned block of 128 entries holds every number of 0 to 127 once.
All inputs are finite; a program needn't handle non-finite values.
Results may differ from a plain program's by a relative error of at most 0.023.
Values may be sent and summed in bfloat16 or wider, within the bound.
A program may use at most 384 MiB of HBM per device.

v0:
```python
import jax
import jax.numpy as jnp
from jax import lax
from jax.sharding import PartitionSpec as P

HEAD_DIM = 128
FF = 5632
NORM_EPSILON = 1e-05
NEGATIVE = -1e30
THETA = 10000.0
HIGH = lax.Precision.HIGHEST


def rotary_tables(length_total, head_size):
    position = jnp.arange(length_total, dtype=jnp.float32)
    frequency = THETA ** (-(jnp.arange(head_size // 2, dtype=jnp.float32) * 2.0 / head_size))
    angles = position[:, None] * frequency[None, :]
    return (jnp.cos(angles)[:, None, :], jnp.sin(angles)[:, None, :])


def rotate(values, cosine, sine):
    half_size = values.shape[-1] // 2
    first = values[..., :half_size]
    second = values[..., half_size:]
    return jnp.concatenate(
        [first * cosine - second * sine, second * cosine + first * sine], axis=-1
    )


def rotate_back(grad_rows, cosine, sine):
    half_size = grad_rows.shape[-1] // 2
    first = grad_rows[..., :half_size]
    second = grad_rows[..., half_size:]
    return jnp.concatenate(
        [first * cosine + second * sine, second * cosine - first * sine], axis=-1
    )


def slot_table(routes, order, valid, capacity):
    row_count = routes.shape[0]
    top_count = routes.shape[1]
    pair_rank = order[:, None] + row_count * jnp.arange(top_count, dtype=jnp.int32)[None, :]
    flat_rank = pair_rank.reshape(-1)
    flat_expert = routes.reshape(-1)
    flat_valid = jnp.broadcast_to(valid[:, None], routes.shape).reshape(-1)
    earlier = (
        (flat_rank[None, :] < flat_rank[:, None])
        & (flat_expert[None, :] == flat_expert[:, None])
        & flat_valid[None, :]
    )
    slot_index = jnp.sum(earlier.astype(jnp.int32), axis=1).reshape(row_count, top_count)
    kept_pair = valid[:, None] & (slot_index < capacity)
    target = routes * capacity + jnp.minimum(slot_index, capacity - 1)
    return (target, kept_pair)


def masked_scores(query, key_rows, allowed):
    scale = query.shape[-1] ** (-0.5)
    raw = jnp.einsum("qhd,khd->hqk", query, key_rows, preferred_element_type=jnp.float32) * scale
    return jnp.where(allowed[None], raw, NEGATIVE)


def fetch_expert(w_gate_up, w_down):
    gate_up_full, down_full = (
        lax.all_gather(w_gate_up, "dp", axis=1, tiled=True),
        lax.all_gather(w_down, "dp", axis=1, tiled=True),
    )
    return (gate_up_full[0], down_full[0])


def contract_first(left, right):
    return lax.dot_general(
        left, right, (((0,), (0,)), ((), ())), preferred_element_type=jnp.float32
    )


def contract_last(left, right):
    return lax.dot_general(
        left, right, (((1,), (1,)), ((), ())), preferred_element_type=jnp.float32
    )


def on_device(
    tokens,
    w_qkv,
    w_out,
    attention_norm_gain,
    gain_ffn,
    w_router,
    w_gate_up,
    w_down,
    lengths,
    routes,
    order,
    cotangent,
):
    group_size = lax.axis_size("expert")
    tok_dev = tokens.shape[0]
    seq_len = tok_dev * group_size
    width = tokens.shape[1]
    top_count = routes.shape[1]
    capacity = tok_dev * top_count // group_size
    head_size = HEAD_DIM
    local_width = w_qkv.shape[2]
    heads_local = local_width // head_size
    ff_width = FF
    qkv_full, out_full, first_norm_gain, gain_two, router_full = (
        lax.all_gather(w_qkv, "dp", axis=1, tiled=True),
        lax.all_gather(w_out, "dp", axis=1, tiled=True),
        lax.all_gather(attention_norm_gain, "dp", axis=0, tiled=True),
        lax.all_gather(gain_ffn, "dp", axis=0, tiled=True),
        lax.all_gather(w_router, "dp", axis=0, tiled=True),
    )
    first_norm_gain = first_norm_gain.astype(jnp.float32)
    gain_two = gain_two.astype(jnp.float32)
    own_start = lax.axis_index("expert") * tok_dev
    own_position = own_start + jnp.arange(tok_dev, dtype=jnp.int32)
    live_own = own_position < lengths[0]
    live_rows = live_own.astype(jnp.float32)[:, None]
    inputs_float = tokens.astype(jnp.float32)
    first_inverse_rms = lax.rsqrt(
        jnp.mean(inputs_float * inputs_float, axis=-1, keepdims=True) + NORM_EPSILON
    )
    input_normalized_hat = inputs_float * first_inverse_rms
    normalized_input = (input_normalized_hat * first_norm_gain).astype(jnp.bfloat16)
    whole = lax.all_gather(normalized_input, "expert", axis=0, tiled=True)
    cosine, sine = rotary_tables(seq_len, head_size)
    projected = jnp.einsum("td,cde->cte", whole, qkv_full, preferred_element_type=jnp.float32)
    query = rotate(projected[0].reshape(seq_len, heads_local, head_size), cosine, sine).astype(
        jnp.bfloat16
    )
    key_rows = rotate(projected[1].reshape(seq_len, heads_local, head_size), cosine, sine).astype(
        jnp.bfloat16
    )
    value = projected[2].astype(jnp.bfloat16).reshape(seq_len, heads_local, head_size)
    position = jnp.arange(seq_len, dtype=jnp.int32)
    live_all = position < lengths[0]
    allowed = (position[None, :] <= position[:, None]) & live_all[None, :]
    scores = masked_scores(query, key_rows, allowed)
    top_score = jnp.max(scores, axis=-1, keepdims=True)
    exponent = jnp.exp(scores - top_score)
    row_total = jnp.sum(exponent, axis=-1, keepdims=True)
    probs = exponent / row_total
    log_total = top_score + jnp.log(row_total)
    probs_low = probs.astype(jnp.bfloat16)
    attended = jnp.einsum("hqk,khd->qhd", probs_low, value, preferred_element_type=jnp.float32)
    attended = attended.reshape(seq_len, local_width).astype(jnp.bfloat16)
    attn_part = jnp.dot(attended, out_full, preferred_element_type=jnp.float32)
    attn_own = lax.psum_scatter(
        attn_part.astype(jnp.bfloat16), "expert", scatter_dimension=0, tiled=True
    ).astype(jnp.float32)
    resid = inputs_float + attn_own
    inverse_two = lax.rsqrt(jnp.mean(resid * resid, axis=-1, keepdims=True) + NORM_EPSILON)
    hhat = resid * inverse_two
    hidden_in = (hhat * gain_two).astype(jnp.bfloat16)
    logits = jnp.dot(hidden_in, router_full, preferred_element_type=jnp.float32)
    chosen = jnp.take_along_axis(logits, routes, axis=1)
    gates = jax.nn.softmax(chosen, axis=1)
    target, kept_pair = slot_table(routes, order, live_own, capacity)
    slot_ids = jnp.arange(group_size * capacity, dtype=jnp.int32)
    pair_hits = (slot_ids[:, None, None] == target[None]) & kept_pair[None]
    select = jnp.sum(pair_hits.astype(jnp.float32), axis=2).astype(jnp.bfloat16)
    sent = jnp.dot(select, hidden_in, preferred_element_type=jnp.float32).astype(jnp.bfloat16)
    received = lax.all_to_all(
        sent.reshape(group_size, capacity, width), "expert", split_axis=0, concat_axis=0, tiled=True
    )
    dispatched = received.reshape(group_size * capacity, width)
    gate_up_full, down_full = fetch_expert(w_gate_up, w_down)
    gate_up = jnp.dot(dispatched, gate_up_full, preferred_element_type=jnp.float32)
    gate = gate_up[:, :ff_width]
    upward = gate_up[:, ff_width:]
    sigmoid = jax.nn.sigmoid(gate)
    activated = (gate * sigmoid * upward).astype(jnp.bfloat16)
    expert_out = jnp.dot(activated, down_full, preferred_element_type=jnp.float32).astype(
        jnp.bfloat16
    )
    returned = lax.all_to_all(
        expert_out.reshape(group_size, capacity, width),
        "expert",
        split_axis=0,
        concat_axis=0,
        tiled=True,
    )
    returned = returned.reshape(group_size * capacity, width)
    moe = jnp.zeros_like(resid)
    picked_rows = []
    for index in range(top_count):
        one_hot = pair_hits[:, :, index].astype(jnp.bfloat16)
        picked = contract_first(one_hot, returned)
        picked_rows.append(picked)
        moe = moe + gates[:, index : index + 1] * picked
    output = (live_rows * (resid + moe)).astype(jnp.bfloat16)
    d_out = live_rows * cotangent.astype(jnp.float32)
    d_gates_list = []
    d_back = jnp.zeros((group_size * capacity, width), jnp.float32)
    for index in range(top_count):
        d_gates_list.append(jnp.sum(d_out * picked_rows[index], axis=-1))
        weighted = (gates[:, index : index + 1] * d_out).astype(jnp.bfloat16)
        d_back = d_back + jnp.dot(
            pair_hits[:, :, index].astype(jnp.bfloat16),
            weighted,
            preferred_element_type=jnp.float32,
        )
    d_gates = jnp.stack(d_gates_list, axis=1)
    d_back = d_back.astype(jnp.bfloat16)
    d_out_rows = lax.all_to_all(
        d_back.reshape(group_size, capacity, width),
        "expert",
        split_axis=0,
        concat_axis=0,
        tiled=True,
    )
    d_out_rows = d_out_rows.reshape(group_size * capacity, width)
    gate_up_back, down_back = fetch_expert(w_gate_up, w_down)
    d_activated = contract_last(d_out_rows, down_back)
    columns = activated
    grad_down = lax.psum_scatter(
        contract_first(columns, d_out_rows), "dp", scatter_dimension=0, tiled=True
    )
    silu_gate = gate * sigmoid
    d_gate = d_activated * upward * sigmoid * (1.0 + gate * (1.0 - sigmoid))
    d_up = d_activated * silu_gate
    d_gate_up = jnp.concatenate([d_gate, d_up], axis=1).astype(jnp.bfloat16)
    columns = dispatched
    grad_gate_up = lax.psum_scatter(
        contract_first(columns, d_gate_up), "dp", scatter_dimension=0, tiled=True
    )
    d_rows = contract_last(d_gate_up, gate_up_back).astype(jnp.bfloat16)
    d_sent = lax.all_to_all(
        d_rows.reshape(group_size, capacity, width),
        "expert",
        split_axis=0,
        concat_axis=0,
        tiled=True,
    )
    d_hidden = contract_first(select, d_sent.reshape(group_size * capacity, width))
    d_chosen = gates * (d_gates - jnp.sum(gates * d_gates, axis=1, keepdims=True))
    expert_ids = jnp.arange(group_size, dtype=jnp.int32)
    route_hits = (routes[:, :, None] == expert_ids[None, None, :]).astype(jnp.float32)
    d_logits = jnp.sum(route_hits * d_chosen[:, :, None], axis=1)
    router_f = router_full.astype(jnp.float32)
    d_hidden = d_hidden + jnp.dot(
        d_logits, router_f.T, precision=HIGH, preferred_element_type=jnp.float32
    )
    router_part = jnp.dot(
        hidden_in.astype(jnp.float32).T,
        d_logits,
        precision=HIGH,
        preferred_element_type=jnp.float32,
    )
    gain_two_part = jnp.sum(d_hidden * hhat, axis=0)
    scaled_two = d_hidden * gain_two
    d_resid = d_out + inverse_two * (
        scaled_two - hhat * jnp.mean(scaled_two * hhat, axis=-1, keepdims=True)
    )
    d_attn = d_resid.astype(jnp.bfloat16)
    whole_grad = lax.all_gather(d_attn, "expert", axis=0, tiled=True)
    out_part = contract_first(attended, whole_grad)
    d_attended = contract_last(whole_grad, out_full).astype(jnp.bfloat16)
    d_heads = d_attended.reshape(seq_len, heads_local, head_size)
    probs = jnp.exp(masked_scores(query, key_rows, allowed) - log_total)
    probs_low = probs.astype(jnp.bfloat16)
    d_value = jnp.einsum(
        "hqk,qhd->khd", probs_low, d_heads, preferred_element_type=jnp.float32
    ).astype(jnp.bfloat16)
    d_probs = jnp.einsum("qhd,khd->hqk", d_heads, value, preferred_element_type=jnp.float32)
    row_delta = jnp.sum(probs * d_probs, axis=-1, keepdims=True)
    d_scores = (probs * (d_probs - row_delta)).astype(jnp.bfloat16)
    scale = head_size ** (-0.5)
    d_query = (
        jnp.einsum("hqk,khd->qhd", d_scores, key_rows, preferred_element_type=jnp.float32) * scale
    )
    d_key = jnp.einsum("hqk,qhd->khd", d_scores, query, preferred_element_type=jnp.float32) * scale
    d_query_pre = (
        rotate_back(d_query, cosine, sine).reshape(seq_len, local_width).astype(jnp.bfloat16)
    )
    d_key_pre = rotate_back(d_key, cosine, sine).reshape(seq_len, local_width).astype(jnp.bfloat16)
    d_projected = jnp.stack([d_query_pre, d_key_pre, d_value.reshape(seq_len, local_width)])
    qkv_part = jnp.einsum("td,cte->cde", whole, d_projected, preferred_element_type=jnp.float32)
    d_normed_part = jnp.einsum(
        "cte,cde->td", d_projected, qkv_full, preferred_element_type=jnp.float32
    )
    grad_normalized = lax.psum_scatter(
        d_normed_part.astype(jnp.bfloat16), "expert", scatter_dimension=0, tiled=True
    ).astype(jnp.float32)
    first_gain_piece = jnp.sum(grad_normalized * input_normalized_hat, axis=0)
    first_scaled_input = grad_normalized * first_norm_gain
    grad_tokens = d_resid + first_inverse_rms * (
        first_scaled_input
        - input_normalized_hat
        * jnp.mean(first_scaled_input * input_normalized_hat, axis=-1, keepdims=True)
    )
    gain_one_sum, gain_two_sum, router_sum = (
        lax.psum(first_gain_piece.astype(jnp.bfloat16), "expert").astype(jnp.float32),
        lax.psum(gain_two_part.astype(jnp.bfloat16), "expert").astype(jnp.float32),
        lax.psum(router_part.astype(jnp.bfloat16), "expert").astype(jnp.float32),
    )
    grad_qkv, grad_out, grad_gain_attn, grad_gain_ffn, grad_router = (
        lax.psum_scatter(qkv_part, "dp", scatter_dimension=1, tiled=True),
        lax.psum_scatter(out_part, "dp", scatter_dimension=1, tiled=True),
        lax.psum_scatter(gain_one_sum, "dp", scatter_dimension=0, tiled=True),
        lax.psum_scatter(gain_two_sum, "dp", scatter_dimension=0, tiled=True),
        lax.psum_scatter(router_sum, "dp", scatter_dimension=0, tiled=True),
    )
    return (
        output,
        grad_tokens.astype(jnp.bfloat16),
        grad_qkv,
        grad_out,
        grad_gain_attn,
        grad_gain_ffn,
        grad_router,
        grad_gate_up[None],
        grad_down[None],
    )


def solution(mesh):
    placed = (
        P(("dp", "expert"), None),
        P(None, "dp", "expert"),
        P("expert", "dp"),
        P("dp"),
        P("dp"),
        P("dp", None),
        P("expert", "dp", None),
        P("expert", "dp", None),
        P("dp"),
        P(("dp", "expert"), None),
        P(("dp", "expert")),
        P(("dp", "expert"), None),
    )
    return jax.shard_map(
        on_device,
        mesh=mesh,
        in_specs=placed,
        out_specs=(
            P(("dp", "expert"), None),
            P(("dp", "expert"), None),
            P(None, "dp", "expert"),
            P("expert", "dp"),
            P("dp"),
            P("dp"),
            P("dp", None),
            P("expert", "dp", None),
            P("expert", "dp", None),
        ),
        check_vma=False,
    )
```

profile of v0, /device:TPU:0, one launch (start us, length us, event | category | flops | bytes accessed | tf_op | source)
XLA Modules:
  0.0 1797.1 jit_solution(4819094658459941075)
XLA Ops:
  9.1 10.3 all-gather
  19.5 2.0 fusion.43
  21.6 2.3 copy.189
  26.2 1.7 fusion.55
  27.9 40.1 %all-gather.9.cloned.1.call-done = bf16[512,2048]{1,0:T(8,128)(2,1)} async-done(((bf16[128,2048]{1,0:T(8,128)(2,1)}), bf16[512,2048]{1,0:T(8,128)(2,1)}) %all-gather.9.cloned.1.call-update) | async-done | bytes 2097168 | tf_op jit(solution)/shard_map/all_gather | solution.py:126
  67.9 47.9 %all-gather.11.cloned.1.call-done = bf16[3,2048,512]{1,2,0:T(8,128)(2,1)} async-done(((bf16[3,256,512]{1,2,0:T(8,128)(2,1)}), bf16[3,2048,512]{1,2,0:T(8,128)(2,1)}) %all-gather.11.cloned.1.call-update) | async-done | bytes 6291472 | tf_op jit(solution)/shard_map/all_gather | solution.py:108
  115.8 6.2 fusion.26
  124.1 1.4 copy.232
  126.4 2.4 copy.234
  131.4 2.6 subtract_convert_fusion.3
  136.1 1.4 copy-done
  138.4 7.5 all-gather.13.cloned.1.call-done
  145.9 4.2 convolution_convert_fusion
  151.4 8.8 all-gather.1
  162.4 31.7 %reduce-scatter.12.cloned.1.call-done = bf16[128,2048]{1,0:T(8,128)(2,1)} async-done(((bf16[512,2048]{1,0:T(8,128)(2,1)}), bf16[128,2048]{1,0:T(8,128)(2,1)}) %reduce-scatter.12.cloned.1.call-update) | async-done | bytes 524304 | tf_op jit(solution)/shard_map/reduce_scatter | solution.py:149
  197.2 28.8 %all_to_all.20 = bf16[4,64,2048]{2,1,0:T(8,128)(2,1)S(1)} all-to-all(bf16[4,64,2048]{2,1,0:T(8,128)(2,1)S(1)} %bitcast.116), channel_id=1, replica_groups=mesh['dp'=8,'expert'=4] {'expert'}, dimensions={0} | all-to-all | bytes 2097152 | tf_op jit(solution)/shard_map/all_to_all | solution.py:164
  226.0 184.1 %all-gather.15.cloned.1.call-done = bf16[1,2048,11264]{2,1,0:T(8,128)(2,1)} async-done(((bf16[1,256,11264]{2,1,0:T(8,128)(2,1)}), bf16[1,2048,11264]{2,1,0:T(8,128)(2,1)}) %all-gather.15.cloned.1.call-update) | async-done | bytes 46137360 | tf_op jit(solution)/shard_map/all_gather | solution.py:65
  410.1 25.9 %fusion.2 = f32[256,11264]{1,0:T(8,128)} fusion(bf16[256,2048]{1,0:T(8,128)(2,1)S(1)} %bitcast.114, bf16[1,2048,11264]{2,1,0:T(8,128)(2,1)} %all-gather.15.cloned.1.call-done), kind=kOutput, calls=%fused_computation.3 | convolution fusion | flops 11811160064 | bytes 58720256 | tf_op jit(solution)/shard_map/dot_general | solution.py:169
  436.0 5.2 multiply_convert_fusion.2
  441.2 87.4 %all-gather.17.cloned.1.call-done = bf16[1,5632,2048]{2,1,0:T(8,128)(2,1)} async-done(((bf16[1,704,2048]{2,1,0:T(8,128)(2,1)}), bf16[1,5632,2048]{2,1,0:T(8,128)(2,1)}) %all-gather.17.cloned.1.call-update) | async-done | bytes 23068688 | tf_op jit(solution)/shard_map/all_gather | solution.py:66
  528.5 12.0 fusion.12
  540.6 4.6 all-to-all-start.1
  545.5 8.9 all_gather.34
  556.3 2.4 gather_fusion
  559.5 1.5 copy.196
  562.2 9.2 all-to-all-done.1
  571.4 1.6 fusion.58
  574.1 2.8 multiply_reduce_fusion.4
  579.3 27.9 %all_to_all.21 = bf16[4,64,2048]{2,1,0:T(8,128)(2,1)S(1)} all-to-all(bf16[4,64,2048]{2,1,0:T(8,128)(2,1)S(1)} %bitcast.119), channel_id=1, replica_groups=mesh['dp'=8,'expert'=4] {'expert'}, dimensions={0} | all-to-all | bytes 2097152 | tf_op jit(solution)/shard_map/all_to_all | solution.py:206
  607.3 25.1 %multiply_convert_fusion.1 = (bf16[256,5632]{1,0:T(8,128)(2,1)}, bf16[256,5632]{1,0:T(8,128)(2,1)}) fusion(f32[256,11264]{1,0:T(8,128)} %fusion.2, bf16[256,2048]{1,0:T(8,128)(2,1)S(1)} %bitcast.120, bf16[1,5632,2048]{2,1,0:T(8,128)(2,1)} %all-gather.17.cloned.1.call-done), kind=kOutput, calls=%fused_computation.11 | convolution fusion | flops 5924323328 | bytes 41418752 | tf_op jit(solution)/shard_map/dot_general | solution.py:78
  632.4 21.1 %fusion.16 = bf16[256,2048]{1,0:T(8,128)(2,1)} fusion(bf16[1,2048,11264]{2,1,0:T(8,128)(2,1)} %all-gather.15.cloned.1.call-done, bf16[256,5632]{1,0:T(8,128)(2,1)} %get-tuple-element.81, bf16[256,5632]{1,0:T(8,128)(2,1)} %get-tuple-element.80), kind=kOutput, calls=%fused_computation.31 | convolution fusion | flops 11823218688 | bytes 52953088 | tf_op jit(solution)/shard_map/dot_general | solution.py:78
  653.6 4.4 all-to-all-start.3
  658.1 24.7 %all-to-all-done.3 = bf16[4,64,2048]{2,1,0:T(8,128)(2,1)} async-done(((bf16[4,64,2048]{2,1,0:T(8,128)(2,1)}), bf16[4,64,2048]{2,1,0:T(8,128)(2,1)}, u32[]{:S(2)}, u32[]{:S(2)}) %all-to-all-start.3) | async-done | bytes 1048608 | tf_op jit(solution)/shard_map/all_to_all | solution.py:229
  682.8 1.6 fusion.82
  684.5 2.0 multiply_reduce_fusion.1
  689.3 43.7 %all-gather.19.cloned.1.call-done = bf16[512,2048]{1,0:T(8,128)(2,1)} async-done(((bf16[128,2048]{1,0:T(8,128)(2,1)}), bf16[512,2048]{1,0:T(8,128)(2,1)}) %all-gather.19.cloned.1.call-update) | async-done | bytes 2097168 | tf_op jit(solution)/shard_map/all_gather | solution.py:257
  733.0 3.6 convolution_convert_fusion.3
  736.7 1.6 fusion.35
  740.6 1.8 fusion.33
  742.4 2.0 fusion.34
  744.4 2.0 copy.213
  746.4 3.3 add_convert_fusion.1
  749.7 1.5 pad_maximum_fusion.10
  751.3 2.0 copy.205
  753.3 2.0 copy.211
  755.4 2.0 copy.209
  757.4 2.0 copy.212
  759.5 8.0 bitcast_convert_fusion
  767.6 1.4 convolution_convert_fusion.2
  768.9 41.3 %reduce-scatter.14.cloned.1.call-done = bf16[128,2048]{1,0:T(8,128)(2,1)} async-done(((bf16[512,2048]{1,0:T(8,128)(2,1)}), bf16[128,2048]{1,0:T(8,128)(2,1)}) %reduce-scatter.14.cloned.1.call-update) | async-done | bytes 524304 | tf_op jit(solution)/shard_map/reduce_scatter | solution.py:283
  810.3 1.5 fusion.45
  811.7 17.1 all-reduce.4
  830.3 10.1 convolution_bitcast_fusion
  840.5 5.0 fusion.80
  845.5 19.3 %fusion.81 = f32[5632,2048]{1,0:T(8,128)} fusion(bf16[256,5632]{1,0:T(8,128)(2,1)S(1)} %multiply_convert_fusion.2, bf16[256,2048]{1,0:T(8,128)(2,1)} %bitcast.121), kind=kOutput, calls=%fused_computation.154 | convolution fusion | flops 5905580032 | bytes 50069504 | tf_op jit(solution)/shard_map/dot_general | solution.py:72
  866.0 43.8 %fusion.9 = f32[2048,11264]{1,0:T(8,128)} fusion(bf16[256,2048]{1,0:T(8,128)(2,1)S(1)} %bitcast.115, bf16[256,5632]{1,0:T(8,128)(2,1)} %get-tuple-element.81, bf16[256,5632]{1,0:T(8,128)(2,1)} %get-tuple-element.80), kind=kOutput, calls=%fused_computation.23 | convolution fusion | flops 11822694400 | bytes 99090432 | tf_op jit(solution)/shard_map/dot_general | solution.py:72
  911.8 23.0 %all-reduce.3 = (f32[2048]{0:T(1024)S(1)}, f32[2048]{0:T(1024)S(1)}) all-reduce(bf16[2048]{0:T(1024)(128)(2,1)S(1)} %get-tuple-element.71, bf16[2048]{0:T(1024)(128)(2,1)S(1)} %get-tuple-element.72), channel_id=6, replica_groups=mesh['dp'=8,'expert'=4] {'dp'}, use_global_device_ids=true, to_apply=%region_21.22.clone | all-reduce | flops 4096 | bytes 24576
  936.1 3.5 fusion.42
  939.6 1.6 copy.230
  941.2 19.7 %reduce-scatter.16.cloned.1.call-done = f32[3,256,512]{1,2,0:T(8,128)} async-done(((f32[3,2048,512]{1,2,0:T(8,128)}), f32[3,256,512]{1,2,0:T(8,128)}) %reduce-scatter.16.cloned.1.call-update) | async-done | bytes 1572880 | tf_op jit(solution)/shard_map/reduce_scatter | solution.py:299
  960.9 3.0 copy.216
  963.9 52.3 %reduce-scatter.18.cloned.1.call-done = f32[512,256]{1,0:T(8,128)} async-done(((f32[512,2048]{1,0:T(8,128)}), f32[512,256]{1,0:T(8,128)}) %reduce-scatter.18.cloned.1.call-update) | async-done | bytes 524304 | tf_op jit(solution)/shard_map/reduce_scatter | solution.py:300
  1016.2 268.8 %reduce-scatter.20.cloned.1.call-done = f32[704,2048]{1,0:T(8,128)} async-done(((f32[5632,2048]{1,0:T(8,128)}), f32[704,2048]{1,0:T(8,128)}) %reduce-scatter.20.cloned.1.call-update) | async-done | bytes 5767184 | tf_op jit(solution)/shard_map/reduce_scatter | solution.py:217
  1285.0 505.4 %reduce-scatter.24.cloned.1.call-done = f32[256,11264]{1,0:T(8,128)} async-done(((f32[2048,11264]{1,0:T(8,128)}), f32[256,11264]{1,0:T(8,128)}) %reduce-scatter.24.cloned.1.call-update) | async-done | bytes 11534352
  (222 shorter events, 36.4 us)
Async XLA Ops:
  7.2 60.7 %all-gather.9.cloned.1.call-start = ((), (), s32[]{:S(2)}) async-start(), calls=%async_computation.11 | async-start | bytes 2621440 | tf_op jit(solution)/shard_map/all_gather | solution.py:126
  8.5 113.6 %copy-start.48 = (f32[128]{0:T(128)}, f32[128]{0:T(128)S(1)}, u32[]{:S(2)}) copy-start(f32[128]{0:T(128)S(1)} %add_rsqrt_fusion.1) | copy-start | bytes 1540
  19.5 102.6 %copy-start.34 = (f32[8,1,256]{2,1,0:T(1,128)}, f32[8,1,256]{2,1,0:T(1,128)S(1)}, u32[]{:S(2)}) copy-start(f32[8,1,256]{2,1,0:T(1,128)S(1)} %convert_element_type.200) | copy-start | bytes 24580
  21.5 94.3 %all-gather.11.cloned.1.call-start = ((), (), s32[]{:S(2)}) async-start(), calls=%async_computation.12 | async-start | bytes 7077888 | tf_op jit(solution)/shard_map/all_gather | solution.py:108
  23.9 122.0 %all-gather.13.cloned.1.call-start = ((), (), s32[]{:S(2)}) async-start(), calls=%async_computation.13 | async-start | bytes 2359296 | tf_op jit(solution)/shard_map/all_gather | solution.py:109
  24.6 169.5 %reduce-scatter.12.cloned.1.call-start = ((), (), s32[]{:S(2)}) async-start(), calls=%async_computation.14 | async-start | bytes 2621440 | tf_op jit(solution)/shard_map/reduce_scatter | solution.py:149
  27.9 103.6 %copy-start.23 = (f32[512,64]{1,0:T(8,128)}, f32[512,64]{1,0:T(8,128)S(1)}, u32[]{:S(2)}) copy-start(f32[512,64]{1,0:T(8,128)S(1)} %get-tuple-element.104) | copy-start | bytes 393220
  124.1 4.7 copy-start.27
  131.4 2.6 copy-start.28
  134.0 2.0 copy-start.12
  134.0 3.4 copy-start.25
  135.4 3.0 copy-start.36
  136.1 2.3 copy-start.38
  138.4 12.4 copy-start.29
  150.1 10.9 copy-start.63
  150.2 11.1 copy-start.40
  150.2 44.0 %copy-start.2 = (bf16[128,2048]{1,0:T(8,128)(2,1)S(1)}, bf16[128,2048]{1,0:T(8,128)(2,1)}, u32[]{:S(2)}) copy-start(bf16[128,2048]{1,0:T(8,128)(2,1)} %param.12) | copy-start | bytes 1572868
  150.2 259.9 %all-gather.15.cloned.1.call-start = ((), (), s32[]{:S(2)}) async-start(), calls=%async_computation.15 | async-start | bytes 51904512 | tf_op jit(solution)/shard_map/all_gather | solution.py:65
  150.8 377.8 %all-gather.17.cloned.1.call-start = ((), (), s32[]{:S(2)}) async-start(), calls=%async_computation.16 | async-start | bytes 25952256 | tf_op jit(solution)/shard_map/all_gather | solution.py:66
  160.2 275.7 %copy-start.30 = (f32[8,1,256]{2,1,0:T(1,128)}, f32[8,1,256]{2,1,0:T(1,128)S(1)}, u32[]{:S(2)}) copy-start(f32[8,1,256]{2,1,0:T(1,128)S(1)} %convert_element_type.201) | copy-start | bytes 24580
  162.1 32.1 %copy-start.50 = (pred[128,2]{0,1:T(4,128)(4,1)}, pred[128,2]{0,1:T(4,128)(4,1)S(1)}, u32[]{:S(2)}) copy-start(pred[128,2]{0,1:T(4,128)(4,1)S(1)} %copy.199) | copy-start | bytes 772
  162.3 273.6 %copy-start.43 = (s32[128,2]{0,1:T(2,128)}, s32[128,2]{0,1:T(2,128)S(1)}, u32[]{:S(2)}) copy-start(s32[128,2]{0,1:T(2,128)S(1)} %multiply_add_fusion.1) | copy-start | bytes 3076
  195.4 240.5 %copy-start.46 = (f32[128]{0:T(128)}, f32[128]{0:T(128)S(1)}, u32[]{:S(2)}) copy-start(f32[128]{0:T(128)S(1)} %add_rsqrt_fusion) | copy-start | bytes 1540
  196.7 213.4 %copy-start.11 = (bf16[128,2048]{1,0:T(8,128)(2,1)}, bf16[128,2048]{1,0:T(8,128)(2,1)S(1)}, u32[]{:S(2)}) copy-start(bf16[128,2048]{1,0:T(8,128)(2,1)S(1)} %multiply_convert_fusion.7) | copy-start | bytes 1572868
  226.0 184.2 %copy-start.20 = (bf16[4,64,2048]{2,1,0:T(8,128)(2,1)}, bf16[4,64,2048]{2,1,0:T(8,128)(2,1)S(1)}, u32[]{:S(2)}) copy-start(bf16[4,64,2048]{2,1,0:T(8,128)(2,1)S(1)} %all_to_all.20) | copy-start | bytes 3145732
  441.2 104.3 %copy-start.60 = (bf16[256,4]{0,1:T(4,128)(2,1)S(1)}, bf16[256,4]{0,1:T(4,128)(2,1)}, u32[]{:S(2)}) copy-start(bf16[256,4]{0,1:T(4,128)(2,1)} %param.17) | copy-start | bytes 6148
  540.6 30.9 %all-to-all-start.1 = ((bf16[4,64,2048]{2,1,0:T(8,128)(2,1)}), bf16[4,64,2048]{2,1,0:T(8,128)(2,1)}, u32[]{:S(2)}, u32[]{:S(2)}) async-start(bf16[4,64,2048]{2,1,0:T(8,128)(2,1)} %bitcast.129), calls=%async_computation.2 | async-start | bytes 2097152 | tf_op jit(solution)/shard_map/all_to_all | solution.py:177
  558.7 19.4 %copy-start.41 = (f32[128]{0:T(128)S(1)}, f32[128]{0:T(128)}, u32[]{:S(2)}) copy-start(f32[128]{0:T(128)} %get-tuple-element.76) | copy-start | bytes 1540
  561.7 15.2 copy-start.59
  571.4 5.5 copy-start.62
  571.4 6.8 copy-start.5
  578.2 29.1 %copy-start.44 = (f32[128,2]{0,1:T(2,128)}, f32[128,2]{0,1:T(2,128)S(1)}, u32[]{:S(2)}) copy-start(f32[128,2]{0,1:T(2,128)S(1)} %get-tuple-element.75) | copy-start | bytes 3076
  578.2 29.1 %copy-start.51 = (f32[128]{0:T(128)}, f32[128]{0:T(128)S(1)}, u32[]{:S(2)}) copy-start(f32[128]{0:T(128)S(1)} %get-tuple-element.102) | copy-start | bytes 1540
  578.2 29.1 %copy-start.53 = (f32[128]{0:T(128)}, f32[128]{0:T(128)S(1)}, u32[]{:S(2)}) copy-start(f32[128]{0:T(128)S(1)} %get-tuple-element.103) | copy-start | bytes 1540
  607.3 25.1 %copy-start.22 = (bf16[4,64,2048]{2,1,0:T(8,128)(2,1)}, bf16[4,64,2048]{2,1,0:T(8,128)(2,1)S(1)}, u32[]{:S(2)}) copy-start(bf16[4,64,2048]{2,1,0:T(8,128)(2,1)S(1)} %all_to_all.21) | copy-start | bytes 3145732
  632.4 25.6 %copy-start.45 = (f32[128,2]{0,1:T(2,128)S(1)}, f32[128,2]{0,1:T(2,128)}, u32[]{:S(2)}) copy-start(f32[128,2]{0,1:T(2,128)} %copy-done.44) | copy-start | bytes 3076
  632.4 25.6 %copy-start.56 = (f32[128]{0:T(128)S(1)}, f32[128]{0:T(128)}, u32[]{:S(2)}) copy-start(f32[128]{0:T(128)} %copy-done.55) | copy-start | bytes 1540
  632.4 25.6 %copy-start.58 = (f32[128]{0:T(128)S(1)}, f32[128]{0:T(128)}, u32[]{:S(2)}) copy-start(f32[128]{0:T(128)} %copy-done.57) | copy-start | bytes 1540
  632.4 25.6 %copy-start.61 = (f32[128]{0:T(128)S(1)}, f32[128]{0:T(128)}, u32[]{:S(2)}) copy-start(f32[128]{0:T(128)} %get-tuple-element.74) | copy-start | bytes 1540
  653.6 30.9 %copy-start.31 = (f32[8,1,256]{2,1,0:T(1,128)S(1)}, f32[8,1,256]{2,1,0:T(1,128)}, u32[]{:S(2)}) copy-start(f32[8,1,256]{2,1,0:T(1,128)} %copy-done.30) | copy-start | bytes 24580
  653.6 30.9 %copy-start.33 = (bf16[2048,4]{0,1:T(4,128)(2,1)S(1)}, bf16[2048,4]{0,1:T(4,128)(2,1)}, u32[]{:S(2)}) copy-start(bf16[2048,4]{0,1:T(4,128)(2,1)} %copy-done.32) | copy-start | bytes 49156
  653.6 30.9 %copy-start.47 = (f32[128]{0:T(128)S(1)}, f32[128]{0:T(128)}, u32[]{:S(2)}) copy-start(f32[128]{0:T(128)} %copy-done.46) | copy-start | bytes 1540
  653.6 34.0 %copy-start.42 = (f32[128]{0:T(128)S(1)}, f32[128]{0:T(128)}, u32[]{:S(2)}) copy-start(f32[128]{0:T(128)} %get-tuple-element.76) | copy-start | bytes 1540
  653.6 29.2 %all-to-all-start.3 = ((bf16[4,64,2048]{2,1,0:T(8,128)(2,1)}), bf16[4,64,2048]{2,1,0:T(8,128)(2,1)}, u32[]{:S(2)}, u32[]{:S(2)}) async-start(bf16[4,64,2048]{2,1,0:T(8,128)(2,1)} %bitcast.130), calls=%async_computation.4 | async-start | bytes 2097152 | tf_op jit(solution)/shard_map/all_to_all | solution.py:229
  658.0 75.1 %all-gather.19.cloned.1.call-start = ((), (), s32[]{:S(2)}) async-start(), calls=%async_computation.17 | async-start | bytes 2621440 | tf_op jit(solution)/shard_map/all_gather | solution.py:257
  682.8 4.7 copy-start.3
  682.8 4.7 copy-start.6
  682.8 6.5 copy-start.37
  682.8 6.5 copy-start.39
  688.8 121.4 %reduce-scatter.14.cloned.1.call-start = ((), (), s32[]{:S(2)}) async-start(), calls=%async_computation.18 | async-start | bytes 2621440 | tf_op jit(solution)/shard_map/reduce_scatter | solution.py:283
  733.0 3.7 copy-start.1
  759.5 50.8 %copy-start.35 = (f32[8,1,256]{2,1,0:T(1,128)S(1)}, f32[8,1,256]{2,1,0:T(1,128)}, u32[]{:S(2)}) copy-start(f32[8,1,256]{2,1,0:T(1,128)} %copy-done.34) | copy-start | bytes 24580
  759.5 50.8 %copy-start.49 = (f32[128]{0:T(128)S(1)}, f32[128]{0:T(128)}, u32[]{:S(2)}) copy-start(f32[128]{0:T(128)} %copy-done.48) | copy-start | bytes 1540
  767.5 172.1 %reduce-scatter.22.cloned.1.call-start = ((), (), s32[]{:S(2)}) async-start(), calls=%async_computation.22 | async-start | bytes 1179648
  830.1 130.8 %reduce-scatter.16.cloned.1.call-start = ((), (), s32[]{:S(2)}) async-start(), calls=%async_computation.19 | async-start | bytes 14155776 | tf_op jit(solution)/shard_map/reduce_scatter | solution.py:299
  840.4 175.8 %reduce-scatter.18.cloned.1.call-start = ((), (), s32[]{:S(2)}) async-start(), calls=%async_computation.20 | async-start | bytes 4718592 | tf_op jit(solution)/shard_map/reduce_scatter | solution.py:300
  845.5 439.5 %reduce-scatter.20.cloned.1.call-start = ((), (), s32[]{:S(2)}) async-start(), calls=%async_computation.21 | async-start | bytes 51904512 | tf_op jit(solution)/shard_map/reduce_scatter | solution.py:217
  864.8 925.6 %reduce-scatter.24.cloned.1.call-start = ((), (), s32[]{:S(2)}) async-start(), calls=%async_computation.23 | async-start | bytes 103809024
  909.9 26.2 %copy-start.4 = (bf16[128,2048]{1,0:T(8,128)(2,1)S(1)}, bf16[128,2048]{1,0:T(8,128)(2,1)}, u32[]{:S(2)}) copy-start(bf16[128,2048]{1,0:T(8,128)(2,1)} %reduce-scatter.12.cloned.1.call-done) | copy-start | bytes 1572868
  909.9 26.2 %copy-start.7 = (bf16[128,2048]{1,0:T(8,128)(2,1)S(1)}, bf16[128,2048]{1,0:T(8,128)(2,1)}, u32[]{:S(2)}) copy-start(bf16[128,2048]{1,0:T(8,128)(2,1)} %param.23) | copy-start | bytes 1572868
  909.9 26.2 %copy-start.9 = (f32[128,2048]{1,0:T(8,128)S(1)}, f32[128,2048]{1,0:T(8,128)}, u32[]{:S(2)}) copy-start(f32[128,2048]{1,0:T(8,128)} %copy-done.8) | copy-start | bytes 3145732
  909.9 26.2 %copy-start.24 = (bf16[128,2048]{1,0:T(8,128)(2,1)S(1)}, bf16[128,2048]{1,0:T(8,128)(2,1)}, u32[]{:S(2)}) copy-start(bf16[128,2048]{1,0:T(8,128)(2,1)} %reduce-scatter.14.cloned.1.call-done) | copy-start | bytes 1572868
  909.9 26.2 %copy-start.52 = (f32[128]{0:T(128)S(1)}, f32[128]{0:T(128)}, u32[]{:S(2)}) copy-start(f32[128]{0:T(128)} %copy-done.51) | copy-start | bytes 1540
  909.9 26.2 %copy-start.54 = (f32[128]{0:T(128)S(1)}, f32[128]{0:T(128)}, u32[]{:S(2)}) copy-start(f32[128]{0:T(128)} %copy-done.53) | copy-start | bytes 1540
  (17 other events, 25.4 us)
Sparse Core Ops, SparseCore 0:
  21.7 46.2 all-gather.8
  70.4 45.3 all-gather.10
  117.7 28.1 all-gather.12
  150.2 43.8 reduce-scatter.11
  196.1 214.0 all-gather.14
  412.0 116.4 all-gather.16
  688.9 44.0 all-gather.18
  767.6 42.5 reduce-scatter.13
  830.2 34.4 reduce-scatter.21
  868.0 92.8 reduce-scatter.15
  964.8 51.3 reduce-scatter.17
  1020.7 264.2 reduce-scatter.19
  1289.2 501.1 reduce-scatter.23
where the time goes:
time: 1810 us; the launch traced here: 1800 us
  waiting for transfers between devices  1370 us (76%)
  matrix products  205 us (11%)
  blocking collectives  125 us (7%)
  local copies, waits for them, and re-layouts  41.6 us (2%)
  other arithmetic  33.2 us (2%)
    unnamed x15, waiting for transfers between devices  507 us
    reduce_scatter x1, waiting for transfers between devices, on_device(): lax.psum_scatter(contract_first(columns, d_out_rows), 'dp', scatter_dimen...  269 us
    all_gather x1, waiting for transfers between devices, fetch_expert(): lax.all_gather(w_gate_up, 'dp', axis=1, tiled=True)  184 us
    all_gather x1, waiting for transfers between devices, fetch_expert(): lax.all_gather(w_down, 'dp', axis=1, tiled=True)  87.4 us
    dot_general x6, matrix products, contract_first(): lax.dot_general(left, right, (((0,), (0,)), ((), ())), preferred_element_...  74.2 us
    reduce_scatter x1, waiting for transfers between devices, on_device(): lax.psum_scatter(out_part, 'dp', scatter_dimension=1, tiled=True)  52.3 us
    dot_general x3, matrix products, contract_last(): lax.dot_general(left, right, (((1,), (1,)), ((), ())), preferred_element_...  49.9 us
    all_gather x1, waiting for transfers between devices, on_device(): lax.all_gather(w_qkv, 'dp', axis=1, tiled=True)  47.9 us
  transfers between devices with their start and end apart: 15, of which 14 were waited for; matrix products, arithmetic and copies ran while one was open for 9% of the time, Pallas kernels for 0%

commit v1 on v0

--- a/solution.py
+++ b/solution.py
@@ -1,7 +1,9 @@
+import functools
 import jax
 import jax.numpy as jnp
 from jax import lax
 from jax.sharding import PartitionSpec as P
+from jax.lax import axis_index, axis_size, ppermute
 
 HEAD_DIM = 128
 FF = 5632
@@ -9,6 +11,22 @@
 NEGATIVE = -1e30
 THETA = 10000.0
 HIGH = lax.Precision.HIGHEST
+
+
+def work_sites(view, row_axis):
+    f_now = axis_size(row_axis)
+    a_next, view_out, n_now = (f_now, axis_index(row_axis), view.shape[1])
+    lower, w1 = (view, 1)
+    while w1 < a_next:
+        formed = tuple(((kk, (kk - w1) % a_next) for kk in range(a_next)))
+        seen_now = ppermute(lower, row_axis, formed)
+        lower = jnp.concatenate([lower, seen_now], axis=1)
+        w1 = 2 * w1
+    b_now = jnp.roll(lower, view_out * n_now, axis=1)
+    return b_now
+
+
+attach_the_set = functools.partial(work_sites, row_axis="dp")
 
 
 def rotary_tables(length_total, head_size):
@@ -62,7 +80,7 @@
 
 def fetch_expert(w_gate_up, w_down):
     gate_up_full, down_full = (
-        lax.all_gather(w_gate_up, "dp", axis=1, tiled=True),
+        attach_the_set(w_gate_up),
         lax.all_gather(w_down, "dp", axis=1, tiled=True),
     )
     return (gate_up_full[0], down_full[0])

time: 1810 us -> 2450 us (1.35)
  blocking collectives: 125 us -> 679 us
  other arithmetic: 33.2 us -> 169 us
  waiting for transfers between devices: 1370 us -> 1310 us
    all_gather x1, blocking collectives: 8.85 us -> 593 us  [on_device(): lax.all_gather(gain_ffn, 'dp', axis=0, tiled=True)]
    all_gather x1, waiting for transfers between devices: 7.5 us -> 240 us  [on_device(): lax.all_gather(w_out, 'dp', axis=1, tiled=True)]
    all_gather x1 -> x0, waiting for transfers between devices: 184 us -> none  [fetch_expert(): lax.all_gather(w_gate_up, 'dp', axis=1, tiled=True)]
    squeeze x0 -> x1, other arithmetic: none -> 107 us  [fetch_expert(): return (gate_up_full[0], down_full[0])]
    all_gather x1, waiting for transfers between devices: 87.4 us -> 0.02 us  [fetch_expert(): lax.all_gather(w_down, 'dp', axis=1, tiled=True)]
    ppermute x0 -> x3, waiting for transfers between devices: none -> 71.7 us  [work_sites(): seen_now = ppermute(lower, row_axis, formed)]
    all_gather x1, waiting for transfers between devices: 40.1 us -> 0.02 us  [on_device(): whole = lax.all_gather(normalized_input, 'expert', axis=0, tiled=True)]
    reduce_scatter x1, waiting for transfers between devices: 31.7 us -> 0.02 us  [on_device(): lax.psum_scatter(attn_part.astype(jnp.bfloat16), 'expert', scatter_dimens...]
  transfers between devices with their start and end apart: 15 -> 18, of which waited for: 14 -> 11; matrix products, arithmetic and copies ran while one was open for 9% -> 12% of each run, Pallas kernels for 0% -> 0%
where the time goes in v1:
time: 2450 us; the launch traced here: 2440 us
  waiting for transfers between devices  1310 us (53%)
  blocking collectives  679 us (28%)
  matrix products  203 us (8%)
  other arithmetic  169 us (7%)
  local copies, waits for them, and re-layouts  43.4 us (2%)
    all_gather x1, blocking collectives, on_device(): lax.all_gather(gain_ffn, 'dp', axis=0, tiled=True)  593 us
    unnamed x14, waiting for transfers between devices  506 us
    reduce_scatter x1, waiting for transfers between devices, on_device(): lax.psum_scatter(contract_first(columns, d_out_rows), 'dp', scatter_dimen...  269 us
    all_gather x1, waiting for transfers between devices, on_device(): lax.all_gather(w_out, 'dp', axis=1, tiled=True)  240 us
    squeeze x1, other arithmetic, fetch_expert(): return (gate_up_full[0], down_full[0])  107 us
    dot_general x6, matrix products, contract_first(): lax.dot_general(left, right, (((0,), (0,)), ((), ())), preferred_element_...  74.1 us
    ppermute x3, waiting for transfers between devices, work_sites(): seen_now = ppermute(lower, row_axis, formed)  71.7 us
    reduce_scatter x1, waiting for transfers between devices, on_device(): lax.psum_scatter(out_part, 'dp', scatter_dimension=1, tiled=True)  52.1 us
  transfers between devices with their start and end apart: 18, of which 11 were waited for; matrix products, arithmetic and copies ran while one was open for 12% of the time, Pallas kernels for 0%

profile of v1, /device:TPU:0, one launch (start us, length us, event | category | flops | bytes accessed | tf_op | source)
XLA Modules:
  0.0 2438.1 jit_solution(13068713858909704740)
XLA Ops:
  7.9 10.3 all-gather
  19.5 2.0 fusion.46
  21.6 2.3 copy.189
  23.9 1.4 collective-permute-start
  25.4 71.7 %collective-permute-done = bf16[1,256,11264]{2,1,0:T(8,128)(2,1)S(1)} collective-permute-done((bf16[1,256,11264]{2,1,0:T(8,128)(2,1)}, bf16[1,256,11264]{2,1,0:T(8,128)(2,1)S(1)}, u32[]{:S(2)}, u32[]{:S(2)}) %collective-permute-start) | collective-permute-done | bytes 5767200 | tf_op jit(solution)/shard_map/ppermute | solution.py:22
  97.0 9.3 pad_maximum_fusion.1
  106.4 1.5 collective-permute-start.1
  109.8 29.6 %all-gather.10.cloned.1.call-done = bf16[3,2048,512]{1,2,0:T(8,128)(2,1)} async-done(((bf16[3,256,512]{1,2,0:T(8,128)(2,1)}), bf16[3,2048,512]{1,2,0:T(8,128)(2,1)}) %all-gather.10.cloned.1.call-update) | async-done | bytes 6291472 | tf_op jit(solution)/shard_map/all_gather | solution.py:126
  139.4 6.2 fusion.29
  148.4 2.1 fusion.80
  150.4 2.4 copy.233
  154.1 2.1 subtract_convert_fusion.3
  161.4 239.9 %all-gather.12.cloned.1.call-done = bf16[512,2048]{1,0:T(8,128)(2,1)} async-done(((bf16[512,256]{1,0:T(8,128)(2,1)}), bf16[512,2048]{1,0:T(8,128)(2,1)}) %all-gather.12.cloned.1.call-update) | async-done | bytes 2097168 | tf_op jit(solution)/shard_map/all_gather | solution.py:127
  401.3 4.3 convolution_convert_fusion
  406.3 19.8 pad_maximum_fusion
  427.3 593.0 %all-gather.1 = bf16[8,1,256]{2,1,0:T(2,128)(2,1)S(1)} all-gather(bf16[1,1,256]{2,1,0:T(2,128)(2,1)S(1)} %reshape.318), channel_id=1, replica_groups=mesh['dp'=8,'expert'=4] {'dp'}, dimensions={0}, use_global_device_ids=true | all-gather | bytes 4608 | tf_op jit(solution)/shard_map/all_gather | solution.py:129
  1027.4 4.8 all-to-all-start
  1032.3 107.0 %fusion.4 = bf16[2048,11264]{1,0:T(8,128)(2,1)} fusion(s32[]{:T(128)S(6)} %select_n.29, bf16[1,256,11264]{2,1,0:T(8,128)(2,1)} %param.20, bf16[1,256,11264]{2,1,0:T(8,128)(2,1)} %copy-done.2, bf16[1,512,11264]{2,1,0:T(8,128)(2,1)} %collective-permute-done.1, bf16[1,1024,11264]{2,1,0:T(8,128)(2,1)} %collective-permute-done.2), kind=kLoop, calls=%fused_computation.13 | loop fusion | flops 369098752 | bytes 92274688 | tf_op jit(solution)/shard_map/squeeze | solution.py:86
  1140.3 23.0 fusion.83
  1163.3 5.2 multiply_convert_fusion.2
  1168.5 12.1 fusion.17
  1180.6 5.1 all-to-all-start.1
  1186.0 8.4 all_gather.30
  1196.3 2.4 gather_fusion
  1199.5 1.5 copy.196
  1202.2 9.2 all-to-all-done.1
  1211.4 1.6 fusion.61
  1214.1 2.8 multiply_reduce_fusion.4
  1219.2 27.7 %all_to_all.20 = bf16[4,64,2048]{2,1,0:T(8,128)(2,1)S(1)} all-to-all(bf16[4,64,2048]{2,1,0:T(8,128)(2,1)S(1)} %bitcast.115), channel_id=1, replica_groups=mesh['dp'=8,'expert'=4] {'expert'}, dimensions={0} | all-to-all | bytes 2097152 | tf_op jit(solution)/shard_map/all_to_all | solution.py:224
  1246.9 25.1 %multiply_convert_fusion.1 = (bf16[256,5632]{1,0:T(8,128)(2,1)}, bf16[256,5632]{1,0:T(8,128)(2,1)}) fusion(f32[256,11264]{1,0:T(8,128)} %fusion.83, bf16[256,2048]{1,0:T(8,128)(2,1)S(1)} %bitcast.116, bf16[1,5632,2048]{2,1,0:T(8,128)(2,1)} %all-gather.14.cloned.1.call-done), kind=kOutput, calls=%fused_computation.25 | convolution fusion | flops 5924323328 | bytes 41418752 | tf_op jit(solution)/shard_map/dot_general | solution.py:96
  1272.1 21.1 fusion.21
  1293.2 4.4 all-to-all-start.3
  1297.7 24.7 %all-to-all-done.3 = bf16[4,64,2048]{2,1,0:T(8,128)(2,1)} async-done(((bf16[4,64,2048]{2,1,0:T(8,128)(2,1)}), bf16[4,64,2048]{2,1,0:T(8,128)(2,1)}, u32[]{:S(2)}, u32[]{:S(2)}) %all-to-all-start.3) | async-done | bytes 1048608 | tf_op jit(solution)/shard_map/all_to_all | solution.py:247
  1322.5 1.6 fusion.86
  1324.1 2.0 multiply_reduce_fusion.1
  1327.1 2.5 fusion.74
  1329.8 43.7 %all-gather.16.cloned.1.call-done = bf16[512,2048]{1,0:T(8,128)(2,1)} async-done(((bf16[128,2048]{1,0:T(8,128)(2,1)}), bf16[512,2048]{1,0:T(8,128)(2,1)}) %all-gather.16.cloned.1.call-update) | async-done | bytes 2097168 | tf_op jit(solution)/shard_map/all_gather | solution.py:275
  1373.5 3.6 convolution_convert_fusion.3
  1377.2 1.6 fusion.38
  1381.1 2.0 fusion.37
  1383.1 1.8 fusion.36
  1384.9 2.0 copy.213
  1386.9 3.3 add_convert_fusion.1
  1390.2 1.5 pad_maximum_fusion.12
  1391.8 2.0 copy.209
  1393.8 2.0 copy.212
  1395.8 2.0 copy.205
  1397.9 2.0 copy.211
  1399.9 8.0 bitcast_convert_fusion
  1409.4 41.3 %reduce-scatter.14.cloned.1.call-done = bf16[128,2048]{1,0:T(8,128)(2,1)} async-done(((bf16[512,2048]{1,0:T(8,128)(2,1)}), bf16[128,2048]{1,0:T(8,128)(2,1)}) %reduce-scatter.14.cloned.1.call-update) | async-done | bytes 524304 | tf_op jit(solution)/shard_map/reduce_scatter | solution.py:301
  1450.7 1.5 fusion.48
  1452.2 17.1 all-reduce.4
  1470.8 10.1 convolution_bitcast_fusion
  1481.0 5.0 fusion.84
  1486.1 19.3 fusion.85
  1506.6 43.8 %fusion.13 = f32[2048,11264]{1,0:T(8,128)} fusion(bf16[256,2048]{1,0:T(8,128)(2,1)S(1)} %bitcast.112, bf16[256,5632]{1,0:T(8,128)(2,1)} %get-tuple-element.82, bf16[256,5632]{1,0:T(8,128)(2,1)} %get-tuple-element.81), kind=kOutput, calls=%fused_computation.37 | convolution fusion | flops 11822694400 | bytes 99090432 | tf_op jit(solution)/shard_map/dot_general | solution.py:90
  1552.3 23.1 all-reduce.3
  1576.7 3.5 fusion.45
  1580.1 1.6 copy.230
  1581.8 19.7 reduce-scatter.16.cloned.1.call-done
  1601.5 3.0 copy.216
  1604.5 52.1 %reduce-scatter.18.cloned.1.call-done = f32[512,256]{1,0:T(8,128)} async-done(((f32[512,2048]{1,0:T(8,128)}), f32[512,256]{1,0:T(8,128)}) %reduce-scatter.18.cloned.1.call-update) | async-done | bytes 524304 | tf_op jit(solution)/shard_map/reduce_scatter | solution.py:318
  1656.6 269.0 %reduce-scatter.20.cloned.1.call-done = f32[704,2048]{1,0:T(8,128)} async-done(((f32[5632,2048]{1,0:T(8,128)}), f32[704,2048]{1,0:T(8,128)}) %reduce-scatter.20.cloned.1.call-update) | async-done | bytes 5767184 | tf_op jit(solution)/shard_map/reduce_scatter | solution.py:235
  1925.6 505.2 %reduce-scatter.24.cloned.1.call-done = f32[256,11264]{1,0:T(8,128)} async-done(((f32[2048,11264]{1,0:T(8,128)}), f32[256,11264]{1,0:T(8,128)}) %reduce-scatter.24.cloned.1.call-update) | async-done | bytes 11534352
  (223 shorter events, 40.1 us)
Async XLA Ops:
  7.2 102.6 %all-gather.8.cloned.1.call-start = ((), (), s32[]{:S(2)}) async-start(), calls=%async_computation.11 | async-start | bytes 2621440 | tf_op jit(solution)/shard_map/all_gather | solution.py:144
  18.2 88.1 %copy-start.32 = (f32[8,1,256]{2,1,0:T(1,128)}, f32[8,1,256]{2,1,0:T(1,128)S(1)}, u32[]{:S(2)}) copy-start(f32[8,1,256]{2,1,0:T(1,128)S(1)} %convert_element_type.200) | copy-start | bytes 24580
  19.5 86.9 %copy-start.45 = (f32[128]{0:T(128)}, f32[128]{0:T(128)S(1)}, u32[]{:S(2)}) copy-start(f32[128]{0:T(128)S(1)} %add_rsqrt_fusion.1) | copy-start | bytes 1540
  21.5 117.8 %all-gather.10.cloned.1.call-start = ((), (), s32[]{:S(2)}) async-start(), calls=%async_computation.12 | async-start | bytes 7077888 | tf_op jit(solution)/shard_map/all_gather | solution.py:126
  23.9 377.4 %all-gather.12.cloned.1.call-start = ((), (), s32[]{:S(2)}) async-start(), calls=%async_computation.13 | async-start | bytes 2359296 | tf_op jit(solution)/shard_map/all_gather | solution.py:127
  23.9 73.1 %collective-permute-start = (bf16[1,256,11264]{2,1,0:T(8,128)(2,1)}, bf16[1,256,11264]{2,1,0:T(8,128)(2,1)S(1)}, u32[]{:S(2)}, u32[]{:S(2)}) collective-permute-start(bf16[1,256,11264]{2,1,0:T(8,128)(2,1)} %param.20), channel_id=1, source_target_pairs={{0,28},{4,0},{8,4},{12,8},{16,12},{20,16},{24,20},{28,24},{1,29},{... | collective-permute-start | bytes 17301512 | tf_op jit(solution)/shard_map/ppermute | solution.py:22
  97.0 9.3 copy-start.2
  106.4 299.9 %collective-permute-start.1 = (bf16[1,512,11264]{2,1,0:T(8,128)(2,1)}, bf16[1,512,11264]{2,1,0:T(8,128)(2,1)}, u32[]{:S(2)}, u32[]{:S(2)}) collective-permute-start(bf16[1,512,11264]{2,1,0:T(8,128)(2,1)} %pad_maximum_fusion.1), channel_id=1, source_target_pairs={{0,24},{4,28},{8,0},{12,4},{16,8},{20,12},{24,16},{28,20},{1,25},{... | collective-permute-start | bytes 34603016 | tf_op jit(solution)/shard_map/ppermute | solution.py:22
  107.9 914.6 %reduce-scatter.12.cloned.1.call-start = ((), (), s32[]{:S(2)}) async-start(), calls=%async_computation.14 | async-start | bytes 2621440 | tf_op jit(solution)/shard_map/reduce_scatter | solution.py:167
  109.7 44.4 %copy-start.22 = (f32[512,64]{1,0:T(8,128)}, f32[512,64]{1,0:T(8,128)S(1)}, u32[]{:S(2)}) copy-start(f32[512,64]{1,0:T(8,128)S(1)} %get-tuple-element.105) | copy-start | bytes 393220
  109.7 44.4 %copy-start.23 = (f32[512,64]{1,0:T(8,128)}, f32[512,64]{1,0:T(8,128)S(1)}, u32[]{:S(2)}) copy-start(f32[512,64]{1,0:T(8,128)S(1)} %get-tuple-element.106) | copy-start | bytes 393220
  156.2 5.2 copy-start.11
  156.2 4.2 copy-start.25
  158.4 3.0 copy-start.34
  161.4 264.7 %copy-start.27 = (bf16[4,128,512]{2,1,0:T(8,128)(2,1)}, bf16[4,128,512]{2,1,0:T(8,128)(2,1)S(1)}, u32[]{:S(2)}) copy-start(bf16[4,128,512]{2,1,0:T(8,128)(2,1)S(1)} %fusion.41) | copy-start | bytes 1572868
  405.6 762.9 %all-gather.14.cloned.1.call-start = ((), (), s32[]{:S(2)}) async-start(), calls=%async_computation.15 | async-start | bytes 25952256 | tf_op jit(solution)/shard_map/all_gather | solution.py:84
  406.2 21.1 copy-start.61
  406.2 614.0 %copy-start.38 = (s32[128,2]{0,1:T(2,128)S(1)}, s32[128,2]{0,1:T(2,128)}, u32[]{:S(2)}) copy-start(s32[128,2]{0,1:T(2,128)} %param.23) | copy-start | bytes 3076
  406.2 614.3 %copy-start.60 = (s32[128]{0:T(128)S(1)}, s32[128]{0:T(128)}, u32[]{:S(2)}) copy-start(s32[128]{0:T(128)} %param.24) | copy-start | bytes 1540
  406.2 616.4 %copy-start.3 = (bf16[128,2048]{1,0:T(8,128)(2,1)S(1)}, bf16[128,2048]{1,0:T(8,128)(2,1)}, u32[]{:S(2)}) copy-start(bf16[128,2048]{1,0:T(8,128)(2,1)} %param.14) | copy-start | bytes 1572868
  426.1 606.2 %collective-permute-start.2 = (bf16[1,1024,11264]{2,1,0:T(8,128)(2,1)}, bf16[1,1024,11264]{2,1,0:T(8,128)(2,1)}, u32[]{:S(2)}, u32[]{:S(2)}) collective-permute-start(bf16[1,1024,11264]{2,1,0:T(8,128)(2,1)} %pad_maximum_fusion), channel_id=1, source_target_pairs={{0,16},{4,20},{8,24},{12,28},{16,0},{20,4},{24,8},{28,12},{1,17},{... | collective-permute-start | bytes 69206024 | tf_op jit(solution)/shard_map/ppermute | solution.py:22
  1020.3 7.1 copy-start.28
  1022.4 5.1 copy-start.41
  1024.0 3.5 copy-start.43
  1027.4 111.9 %all-to-all-start = ((bf16[4,64,2048]{2,1,0:T(8,128)(2,1)}), bf16[4,64,2048]{2,1,0:T(8,128)(2,1)S(1)}, u32[]{:S(2)}, u32[]{:S(2)}) async-start(bf16[4,64,2048]{2,1,0:T(8,128)(2,1)} %bitcast.13), calls=%async_computation.1 | async-start | bytes 2097152 | tf_op jit(solution)/shard_map/all_to_all | solution.py:182
  1168.5 17.5 copy-start.57
  1168.5 25.8 %copy-start.42 = (s32[128,2]{0,1:T(2,128)S(1)}, s32[128,2]{0,1:T(2,128)}, u32[]{:S(2)}) copy-start(s32[128,2]{0,1:T(2,128)} %copy-done.41) | copy-start | bytes 3076
  1180.6 30.8 %all-to-all-start.1 = ((bf16[4,64,2048]{2,1,0:T(8,128)(2,1)}), bf16[4,64,2048]{2,1,0:T(8,128)(2,1)}, u32[]{:S(2)}, u32[]{:S(2)}) async-start(bf16[4,64,2048]{2,1,0:T(8,128)(2,1)} %bitcast.125), calls=%async_computation.2 | async-start | bytes 2097152 | tf_op jit(solution)/shard_map/all_to_all | solution.py:195
  1198.7 19.4 copy-start.39
  1201.7 15.2 copy-start.56
  1211.4 5.5 copy-start.59
  1211.4 6.7 copy-start.5
  1218.1 28.8 %copy-start.50 = (f32[128]{0:T(128)}, f32[128]{0:T(128)S(1)}, u32[]{:S(2)}) copy-start(f32[128]{0:T(128)S(1)} %get-tuple-element.104) | copy-start | bytes 1540
  1218.1 53.9 %copy-start.48 = (f32[128]{0:T(128)}, f32[128]{0:T(128)S(1)}, u32[]{:S(2)}) copy-start(f32[128]{0:T(128)S(1)} %get-tuple-element.103) | copy-start | bytes 1540
  1246.9 25.1 %copy-start.21 = (bf16[4,64,2048]{2,1,0:T(8,128)(2,1)}, bf16[4,64,2048]{2,1,0:T(8,128)(2,1)S(1)}, u32[]{:S(2)}) copy-start(bf16[4,64,2048]{2,1,0:T(8,128)(2,1)S(1)} %all_to_all.20) | copy-start | bytes 3145732
  1272.0 25.6 %copy-start.53 = (f32[128]{0:T(128)S(1)}, f32[128]{0:T(128)}, u32[]{:S(2)}) copy-start(f32[128]{0:T(128)} %copy-done.52) | copy-start | bytes 1540
  1272.1 25.6 %copy-start.55 = (f32[128]{0:T(128)S(1)}, f32[128]{0:T(128)}, u32[]{:S(2)}) copy-start(f32[128]{0:T(128)} %copy-done.54) | copy-start | bytes 1540
  1272.1 25.6 %copy-start.58 = (f32[128]{0:T(128)S(1)}, f32[128]{0:T(128)}, u32[]{:S(2)}) copy-start(f32[128]{0:T(128)} %get-tuple-element.75) | copy-start | bytes 1540
  1272.1 52.0 %copy-start.29 = (f32[8,1,256]{2,1,0:T(1,128)S(1)}, f32[8,1,256]{2,1,0:T(1,128)}, u32[]{:S(2)}) copy-start(f32[8,1,256]{2,1,0:T(1,128)} %copy-done.28) | copy-start | bytes 24580
  1272.1 52.0 %copy-start.31 = (bf16[2048,4]{0,1:T(4,128)(2,1)S(1)}, bf16[2048,4]{0,1:T(4,128)(2,1)}, u32[]{:S(2)}) copy-start(bf16[2048,4]{0,1:T(4,128)(2,1)} %copy-done.30) | copy-start | bytes 49156
  1272.1 52.0 %copy-start.44 = (f32[128]{0:T(128)S(1)}, f32[128]{0:T(128)}, u32[]{:S(2)}) copy-start(f32[128]{0:T(128)} %copy-done.43) | copy-start | bytes 1540
  1293.2 36.6 %copy-start.35 = (f32[4,512]{1,0:T(4,128)S(1)}, f32[4,512]{1,0:T(4,128)}, u32[]{:S(2)}) copy-start(f32[4,512]{1,0:T(4,128)} %copy-done.34) | copy-start | bytes 24580
  1293.2 36.6 %copy-start.37 = (f32[4,512]{1,0:T(4,128)S(1)}, f32[4,512]{1,0:T(4,128)}, u32[]{:S(2)}) copy-start(f32[4,512]{1,0:T(4,128)} %copy-done.36) | copy-start | bytes 24580
  1293.2 29.2 %all-to-all-start.3 = ((bf16[4,64,2048]{2,1,0:T(8,128)(2,1)}), bf16[4,64,2048]{2,1,0:T(8,128)(2,1)}, u32[]{:S(2)}, u32[]{:S(2)}) async-start(bf16[4,64,2048]{2,1,0:T(8,128)(2,1)} %bitcast.126), calls=%async_computation.4 | async-start | bytes 2097152 | tf_op jit(solution)/shard_map/all_to_all | solution.py:247
  1297.6 75.9 %all-gather.16.cloned.1.call-start = ((), (), s32[]{:S(2)}) async-start(), calls=%async_computation.16 | async-start | bytes 2621440 | tf_op jit(solution)/shard_map/all_gather | solution.py:275
  1329.6 121.2 %reduce-scatter.14.cloned.1.call-start = ((), (), s32[]{:S(2)}) async-start(), calls=%async_computation.17 | async-start | bytes 2621440 | tf_op jit(solution)/shard_map/reduce_scatter | solution.py:301
  1373.5 3.7 copy-start.1
  1373.5 5.3 copy-start.26
  1379.8 3.3 copy-start.12
  1379.8 3.3 copy-start.14
  1399.9 50.8 %copy-start.33 = (f32[8,1,256]{2,1,0:T(1,128)S(1)}, f32[8,1,256]{2,1,0:T(1,128)}, u32[]{:S(2)}) copy-start(f32[8,1,256]{2,1,0:T(1,128)} %copy-done.32) | copy-start | bytes 24580
  1399.9 50.8 %copy-start.46 = (f32[128]{0:T(128)S(1)}, f32[128]{0:T(128)}, u32[]{:S(2)}) copy-start(f32[128]{0:T(128)} %copy-done.45) | copy-start | bytes 1540
  1408.0 172.1 %reduce-scatter.22.cloned.1.call-start = ((), (), s32[]{:S(2)}) async-start(), calls=%async_computation.21 | async-start | bytes 1179648
  1470.6 131.0 %reduce-scatter.16.cloned.1.call-start = ((), (), s32[]{:S(2)}) async-start(), calls=%async_computation.18 | async-start | bytes 14155776 | tf_op jit(solution)/shard_map/reduce_scatter | solution.py:317
  1480.9 175.7 %reduce-scatter.18.cloned.1.call-start = ((), (), s32[]{:S(2)}) async-start(), calls=%async_computation.19 | async-start | bytes 4718592 | tf_op jit(solution)/shard_map/reduce_scatter | solution.py:318
  1486.0 439.6 %reduce-scatter.20.cloned.1.call-start = ((), (), s32[]{:S(2)}) async-start(), calls=%async_computation.20 | async-start | bytes 51904512 | tf_op jit(solution)/shard_map/reduce_scatter | solution.py:235
  1505.4 925.5 %reduce-scatter.24.cloned.1.call-start = ((), (), s32[]{:S(2)}) async-start(), calls=%async_computation.22 | async-start | bytes 103809024
  1550.4 26.2 %copy-start.4 = (bf16[128,2048]{1,0:T(8,128)(2,1)S(1)}, bf16[128,2048]{1,0:T(8,128)(2,1)}, u32[]{:S(2)}) copy-start(bf16[128,2048]{1,0:T(8,128)(2,1)} %reduce-scatter.12.cloned.1.call-done) | copy-start | bytes 1572868
  1550.4 26.2 %copy-start.6 = (bf16[128,2048]{1,0:T(8,128)(2,1)S(1)}, bf16[128,2048]{1,0:T(8,128)(2,1)}, u32[]{:S(2)}) copy-start(bf16[128,2048]{1,0:T(8,128)(2,1)} %param.25) | copy-start | bytes 1572868
  1550.4 26.2 %copy-start.8 = (f32[128,2048]{1,0:T(8,128)S(1)}, f32[128,2048]{1,0:T(8,128)}, u32[]{:S(2)}) copy-start(f32[128,2048]{1,0:T(8,128)} %copy-done.7) | copy-start | bytes 3145732
  1550.4 26.2 %copy-start.24 = (bf16[128,2048]{1,0:T(8,128)(2,1)S(1)}, bf16[128,2048]{1,0:T(8,128)(2,1)}, u32[]{:S(2)}) copy-start(bf16[128,2048]{1,0:T(8,128)(2,1)} %reduce-scatter.14.cloned.1.call-done) | copy-start | bytes 1572868
  1550.4 26.2 %copy-start.40 = (f32[128]{0:T(128)S(1)}, f32[128]{0:T(128)}, u32[]{:S(2)}) copy-start(f32[128]{0:T(128)} %get-tuple-element.77) | copy-start | bytes 1540
  1550.4 26.2 %copy-start.49 = (f32[128]{0:T(128)S(1)}, f32[128]{0:T(128)}, u32[]{:S(2)}) copy-start(f32[128]{0:T(128)} %copy-done.48) | copy-start | bytes 1540
  1550.4 26.2 %copy-start.51 = (f32[128]{0:T(128)S(1)}, f32[128]{0:T(128)}, u32[]{:S(2)}) copy-start(f32[128]{0:T(128)} %copy-done.50) | copy-start | bytes 1540
  (17 other events, 21.7 us)
Sparse Core Ops, SparseCore 0:
  21.7 46.2 all-gather.7
  70.4 68.9 all-gather.9
  141.2 260.0 all-gather.11
  405.7 43.8 reduce-scatter.11
  451.5 208.7 all-gather.13
  1329.7 43.7 all-gather.15
  1408.1 42.5 reduce-scatter.13
  1470.7 34.3 reduce-scatter.21
  1508.6 92.8 reduce-scatter.15
  1605.3 51.2 reduce-scatter.17
  1661.3 264.3 reduce-scatter.19
  1929.7 501.1 reduce-scatter.23
